TPU v7x, 32 devices: a whole 2x2x4 slice. The times are simulated.
32 devices in a mesh: ctx: 8 (over z, y), grp: 4 (over x, core).
Axes of the slice: x: 2, y: 2, z: 4, core: 2. Of those that a mesh axis runs over, the one named last changes fastest.
Arguments:
- tokens: bfloat16 [4, 512, 8192], P('grp', 'ctx'), may hold values from -6 to 6
- queries: bfloat16 [4, 512, 4096], P('grp', 'ctx'), may hold values from -32 to 32
- key_value_weight: bfloat16 [8192, 1024], P('grp'), may hold values from -0.0625 to 0.0625
- adapter_down_weight: bfloat16 [8192, 128], P('grp'), may hold values from -0.0625 to 0.0625
- adapter_up_weight: bfloat16 [2, 64, 512], replicated, may hold values from -0.75 to 0.75
- tile_request_mask: int32 [4, 4, 4], P('grp'), may hold values 0 or 1
- lengths: int32 [4], P('grp'), may hold values from 128 to 512, as said below
- page_lookup_table: int32 [4, 128], P(None, 'ctx'), may hold values from 0 to 63, as said below
Outputs:
- attended: bfloat16 [4, 512, 4096], P('grp', 'ctx')
- decode_cache: bfloat16 [4, 128, 4, 1024], P('grp', 'ctx')
Inputs may be any that keep to these rules, and one draw needn't show every extreme that they name: `page_lookup_table`: pages of positions held by one index of ctx go to decode-cache rows of that same index. Every decode group receives exactly 16 pages into distinct slots from the pages of each index of ctx. From the pages of one rollout on one index of ctx, at most max(2, ceil(4)) go to one group, and exactly that many to some group. `lengths`: some rollout has all 512 positions live.
All inputs are finite; a program needn't handle non-finite values. No bound on the sum of `tile_request_mask` on one device may be relied on, other than what follows from the above.
Results may differ from a plain program's by a relative error of at most 0.028.
Values may be sent and summed in bfloat16 or wider, within the bound.
A program may use at most 64 MiB of HBM per device.

v0:
```python
import jax
import jax.numpy as jnp
from jax import lax
from jax.sharding import PartitionSpec as P

HEAD_SIZE = 128
HQ = 32
KEY_VALUE_HEADS = 4
PAGE = 4
TILE = 128
THETA = 500000.0
ADAPTER_SCALE = 0.5


def rotate(key_rows, token_positions):
    half_split = HEAD_SIZE // 2
    freq = THETA ** (-(2.0 * jnp.arange(half_split, dtype=jnp.float32)) / HEAD_SIZE)
    angle = token_positions.astype(jnp.float32)[:, None] * freq[None, :]
    cosine = jnp.cos(angle)[:, None, :]
    sine = jnp.sin(angle)[:, None, :]
    first = key_rows[..., :half_split]
    second = key_rows[..., half_split:]
    return jnp.concatenate([first * cosine - second * sine, second * cosine + first * sine], -1)


def send_pages(own, page_lookup_table, groups):
    column_width = own.shape[1]
    ppd = own.shape[0] // PAGE
    most = max(2, -(-ppd // groups))
    me = lax.axis_index("grp")
    dest = page_lookup_table // ppd
    slot = page_lookup_table % ppd
    earlier = jnp.arange(ppd)[:, None] > jnp.arange(ppd)[None, :]
    same = dest[:, :, None] == dest[:, None, :]
    order = jnp.sum(same & earlier[None], axis=2)
    my_dest = lax.dynamic_index_in_dim(dest, me, 0, keepdims=False)
    my_order = lax.dynamic_index_in_dim(order, me, 0, keepdims=False)
    pick = (my_dest[None, None, :] == jnp.arange(groups)[:, None, None]) & (
        my_order[None, None, :] == jnp.arange(most)[None, :, None]
    )
    pages = own.reshape(ppd, PAGE * column_width)
    outgoing = jnp.einsum(
        "gck,kf->gcf", pick.astype(jnp.bfloat16), pages, preferred_element_type=jnp.float32
    ).astype(jnp.bfloat16)
    incoming = lax.all_to_all(outgoing, "grp", split_axis=0, concat_axis=0, tiled=True)
    place = (
        (dest[None, :, None, :] == me)
        & (order[None, :, None, :] == jnp.arange(most)[None, None, :, None])
        & (slot[None, :, None, :] == jnp.arange(ppd)[:, None, None, None])
    )
    place = jnp.any(place, axis=3).reshape(ppd, groups * most)
    cache = jnp.dot(
        place.astype(jnp.bfloat16),
        incoming.reshape(groups * most, PAGE * column_width),
        preferred_element_type=jnp.float32,
    )
    return cache.astype(jnp.bfloat16).reshape(1, ppd, PAGE, column_width)


def local(
    tokens,
    queries,
    key_value_weight,
    adapter_down_weight,
    adapter_up_weight,
    tile_request_mask,
    lengths,
    page_lookup_table,
):
    groups = lax.axis_size("grp")
    tok = tokens.shape[1]
    column_width = key_value_weight.shape[1]
    half_split = column_width // 2
    rank_count = adapter_up_weight.shape[1]
    group = HQ // KEY_VALUE_HEADS
    ctx_pos = lax.axis_index("ctx")
    token_positions = ctx_pos * tok + jnp.arange(tok, dtype=jnp.int32)
    mixed_output = lax.all_to_all(tokens[0], "grp", split_axis=1, concat_axis=0, tiled=True)
    summed_output = lax.psum_scatter(
        jnp.concatenate(
            [
                jnp.dot(mixed_output, key_value_weight, preferred_element_type=jnp.float32),
                jnp.dot(mixed_output, adapter_down_weight, preferred_element_type=jnp.float32),
            ],
            1,
        ).astype(jnp.bfloat16),
        "grp",
        scatter_dimension=0,
        tiled=True,
    ).astype(jnp.float32)
    low_rank_state = summed_output[:, column_width:].astype(jnp.bfloat16)
    key_rows = summed_output[:, :half_split] + ADAPTER_SCALE * jnp.dot(
        low_rank_state[:, :rank_count], adapter_up_weight[0], preferred_element_type=jnp.float32
    )
    value_rows = summed_output[:, half_split:column_width] + ADAPTER_SCALE * jnp.dot(
        low_rank_state[:, rank_count:], adapter_up_weight[1], preferred_element_type=jnp.float32
    )
    key_rows = rotate(key_rows.reshape(tok, KEY_VALUE_HEADS, HEAD_SIZE), token_positions).reshape(
        tok, half_split
    )
    own = jnp.concatenate([key_rows, value_rows], 1).astype(jnp.bfloat16)
    decode_cache = send_pages(own, page_lookup_table, groups)
    query_heads = queries[0].reshape(tok, KEY_VALUE_HEADS, group, HEAD_SIZE)
    scale = 1.0 / HEAD_SIZE**0.5
    tiles = tile_request_mask.shape[1]
    tile_ids = jnp.arange(tiles, dtype=jnp.int32)
    query_tile = token_positions // TILE
    query_onehot = (query_tile[:, None] == tile_ids[None, :]).astype(jnp.float32)
    live_rows = jnp.dot(query_onehot, tile_request_mask[0].astype(jnp.float32))
    length = lengths[0]
    initial = (
        jnp.full((KEY_VALUE_HEADS, group, tok, 1), -1e30, jnp.float32),
        jnp.zeros((KEY_VALUE_HEADS, group, tok, 1), jnp.float32),
        jnp.zeros((KEY_VALUE_HEADS, group, tok, HEAD_SIZE), jnp.float32),
    )
    state = initial
    piece = lax.all_gather(own, "ctx", axis=0, tiled=True)
    count = piece.shape[0]
    blk = 512
    blocks = piece.reshape(count // blk, blk, column_width)

    def inner(carry, item):
        offset, block = item
        peak, total, acc = carry
        kpos = offset * blk + jnp.arange(blk, dtype=jnp.int32)
        key_block = block[:, :half_split].reshape(blk, KEY_VALUE_HEADS, HEAD_SIZE)
        value_block = (
            block[:, half_split:].reshape(blk, KEY_VALUE_HEADS, HEAD_SIZE).astype(jnp.float32)
        )
        score = (
            jnp.einsum("qhgd,khd->hgqk", query_heads, key_block, preferred_element_type=jnp.float32)
            * scale
        )
        key_tile = kpos // TILE
        key_onehot = (key_tile[:, None] == tile_ids[None, :]).astype(jnp.float32)
        live = jnp.dot(live_rows, key_onehot.T) > 0.5
        live = live | (query_tile[:, None] == key_tile[None, :])
        allowed = (kpos[None, :] <= token_positions[:, None]) & (kpos[None, :] >= 0) & live & (
            kpos[None, :] < length
        ) | (kpos[None, :] == token_positions[:, None])
        masked = jnp.where(allowed, score, -1e30)
        new_peak = jnp.maximum(peak, jnp.max(masked, axis=-1, keepdims=True))
        expo = jnp.where(allowed, jnp.exp(masked - new_peak), 0.0)
        factor = jnp.exp(peak - new_peak)
        total = total * factor + jnp.sum(expo, axis=-1, keepdims=True)
        acc = acc * factor + jnp.einsum(
            "hgqk,khd->hgqd", expo, value_block, preferred_element_type=jnp.float32
        )
        return ((new_peak, total, acc), None)

    offsets = jnp.arange(count // blk, dtype=jnp.int32)
    state, _ = lax.scan(inner, state, (offsets, blocks))
    peak, total, acc = state
    out = acc / total
    out = jnp.transpose(out, (2, 0, 1, 3)).reshape(tok, HQ * HEAD_SIZE)
    out = jnp.where((token_positions < length)[:, None], out, 0.0)
    attended = out.astype(jnp.bfloat16)[None]
    return (attended, decode_cache)


def solution(mesh):
    in_specs = (
        P("grp", "ctx", None),
        P("grp", "ctx", None),
        P("grp", None),
        P("grp", None),
        P(),
        P("grp", None, None),
        P("grp"),
        P(None, "ctx"),
    )
    out_specs = (P("grp", "ctx", None), P("grp", "ctx", None, None))
    return jax.shard_map(local, mesh=mesh, in_specs=in_specs, out_specs=out_specs, check_vma=False)
```

profile of v0, /device:TPU:0, one launch (start us, length us, event | category | flops | bytes accessed | tf_op | source)
XLA Modules:
  0.0 115.5 jit_solution(12051520847819461086)
XLA Ops:
  7.2 0.0 copy-start
  7.2 1.9 %all_to_all.17 = bf16[64,4,2048]{2,1,0:T(4,128)(2,1)S(1)} reshape(bf16[1,64,8192]{2,1,0:T(8,128)(2,1)} %param.8) | data formatting | bytes 2097152 | tf_op jit(solution)/shard_map/all_to_all | solution.py:78
  9.1 1.5 %copy.31 = bf16[64,4,2048]{2,0,1:T(8,128)(2,1)} copy(bf16[64,4,2048]{2,1,0:T(4,128)(2,1)S(1)} %all_to_all.17) | data formatting | bytes 2097152 | tf_op jit(solution)/shard_map/all_to_all | solution.py:78
  10.6 4.2 %all-to-all-start = ((bf16[64,4,2048]{2,0,1:T(8,128)(2,1)}), bf16[64,4,2048]{2,0,1:T(8,128)(2,1)S(1)}, u32[]{:S(2)}, u32[]{:S(2)}) async-start(bf16[64,4,2048]{2,0,1:T(8,128)(2,1)} %copy.31), calls=%async_computation | async-start | bytes 2097152 | tf_op jit(solution)/shard_map/all_to_all | solution.py:78
  14.8 0.0 reduce-scatter.2.cloned.1.call-start
  14.9 14.4 %all-to-all-done = bf16[64,4,2048]{2,0,1:T(8,128)(2,1)S(1)} async-done(((bf16[64,4,2048]{2,0,1:T(8,128)(2,1)}), bf16[64,4,2048]{2,0,1:T(8,128)(2,1)S(1)}, u32[]{:S(2)}, u32[]{:S(2)}) %all-to-all-start) | async-done | bytes 1048608 | tf_op jit(solution)/shard_map/all_to_all | solution.py:78
  29.3 0.0 copy-done
  29.3 0.4 convolution_convert_fusion.2
  29.7 0.0 copy-start.3
  29.8 0.0 copy-start.2
  29.8 0.0 copy-start.1
  29.8 3.5 %convolution_convert_fusion.1 = bf16[256,1024]{1,0:T(8,128)(2,1)S(1)} fusion(bf16[256,2048]{1,0:T(8,128)(2,1)S(1)} %bitcast.71, bf16[2048,1024]{1,0:T(8,128)(2,1)} %param.10), kind=kOutput, calls=%fused_computation.15 | convolution fusion | flops 1074003968 | bytes 5767168 | tf_op jit(solution)/shard_map/dot_general | solution.py:82
  33.3 0.0 copy-start.4
  33.3 0.9 pad_maximum_fusion
  34.2 0.0 reduce-scatter.2.cloned.1.call-update
  34.2 0.0 all-gather.2.cloned.1.call-start
  34.9 0.0 copy-done.3
  35.0 0.2 convert_reduce_fusion
  35.2 0.2 multiply_cosine_fusion
  35.4 22.0 %reduce-scatter.2.cloned.1.call-done = bf16[64,1152]{1,0:T(8,128)(2,1)} async-done(((bf16[256,1152]{1,0:T(8,128)(2,1)}), bf16[64,1152]{1,0:T(8,128)(2,1)}) %reduce-scatter.2.cloned.1.call-update) | async-done | bytes 147472 | tf_op jit(solution)/shard_map/reduce_scatter | solution.py:79
  57.4 0.9 convert_element_type.53
  58.4 0.0 copy-done.2
  58.4 0.9 fusion.12
  59.3 0.2 multiply_subtract_fusion
  59.5 0.1 pad_maximum_fusion.1
  59.6 0.9 fusion.11
  60.5 0.7 maximum_convert_fusion
  61.2 0.0 all-gather.2.cloned.1.call-update
  61.2 0.0 copy-done.1
  61.2 0.1 copy.45
  61.4 0.4 and_reduce_fusion
  61.8 0.4 fusion.16
  62.2 1.0 reshape.298
  63.2 0.8 convolution_convert_fusion
  64.1 3.3 %all-to-all-start.1 = ((bf16[4,4,4096]{2,1,0:T(4,128)(2,1)}), bf16[4,4,4096]{2,1,0:T(4,128)(2,1)S(1)}, u32[]{:S(2)}, u32[]{:S(2)}) async-start(bf16[4,4,4096]{2,1,0:T(4,128)(2,1)} %convolution_convert_fusion), calls=%async_computation.2 | async-start | bytes 262144 | tf_op jit(solution)/shard_map/all_to_all | solution.py:45
  67.4 4.6 %all-to-all-done.1 = bf16[4,4,4096]{2,1,0:T(4,128)(2,1)S(1)} async-done(((bf16[4,4,4096]{2,1,0:T(4,128)(2,1)}), bf16[4,4,4096]{2,1,0:T(4,128)(2,1)S(1)}, u32[]{:S(2)}, u32[]{:S(2)}) %all-to-all-start.1) | async-done | bytes 131104 | tf_op jit(solution)/shard_map/all_to_all | solution.py:45
  72.0 0.2 fusion
  72.2 0.7 reshape.295
  73.0 28.6 %all-gather.2.cloned.1.call-done = bf16[512,1024]{1,0:T(8,128)(2,1)} async-done(((bf16[64,1024]{1,0:T(8,128)(2,1)}), bf16[512,1024]{1,0:T(8,128)(2,1)}) %all-gather.2.cloned.1.call-update) | async-done | bytes 1048592 | tf_op jit(solution)/shard_map/all_gather | solution.py:117
  101.6 1.3 %fusion.49 = (bf16[512,512]{1,0:T(8,128)(2,1)S(1)}, bf16[512,512]{1,0:T(8,128)(2,1)S(1)}) fusion(bf16[512,1024]{1,0:T(8,128)(2,1)} %all-gather.2.cloned.1.call-done), kind=kLoop, calls=%fused_computation.99 | loop fusion | bytes 2097152 | tf_op jit(solution)/shard_map/while/body/eval_jaxpr/slice | solution.py:128
  102.9 0.1 reshape.293
  103.0 0.1 reshape.292
  103.1 1.0 fusion.1
  104.2 1.3 %fusion.2 = f32[4,8,64]{2,1,0:T(8,128)S(1)} fusion(f32[4,512,64,8]{1,2,3,0:T(8,128)S(1)} %get-tuple-element.46, f32[4,8,64]{2,1,0:T(8,128)S(1)} %get-tuple-element.31, pred[64,512]{1,0:T(8,128)(4,1)S(1)} %fusion.16), kind=kLoop, calls=%fused_computation.6 | loop fusion | flops 5240832 | bytes 4243456 | tf_op jit(solution)/shard_map/while/body/eval_jaxpr/reduce_sum | solution.py:145
  105.5 1.6 %fusion.19 = bf16[64,4,8,128]{3,0,2,1:T(8,128)(2,1)S(1)} fusion(f32[4,512,64,8]{1,2,3,0:T(8,128)S(1)} %get-tuple-element.46, f32[4,8,64]{2,1,0:T(8,128)S(1)} %get-tuple-element.31, pred[64,512]{1,0:T(8,128)(4,1)S(1)} %fusion.16, bf16[512,4,128,1]{2,1,0,3:T(4,128)(2,1)S(1)} %bitcast.74, f32[64,4,8]{0,2,1:T(8,128)S(1)} %bitcast_add_fusion, ...), kind=kOutput, calls=%fused_computation.28 | convolution fusion | flops 273416192 | bytes 5300224 | tf_op jit(solution)/shard_map/while/body/eval_jaxpr/hgqk,khd->hgqd/dot_general | solution.py:146
  107.1 0.3 copy.36
  107.5 0.2 reshape.294
  107.7 1.0 select_convert_fusion
  (19 shorter events, 0.2 us)
Async XLA Ops:
  7.2 22.1 %copy-start = (bf16[2048,128]{1,0:T(8,128)(2,1)S(1)}, bf16[2048,128]{1,0:T(8,128)(2,1)}, u32[]{:S(2)}) copy-start(bf16[2048,128]{1,0:T(8,128)(2,1)} %param.11) | copy-start | bytes 1572868
  10.6 18.7 %all-to-all-start = ((bf16[64,4,2048]{2,0,1:T(8,128)(2,1)}), bf16[64,4,2048]{2,0,1:T(8,128)(2,1)S(1)}, u32[]{:S(2)}, u32[]{:S(2)}) async-start(bf16[64,4,2048]{2,0,1:T(8,128)(2,1)} %copy.31), calls=%async_computation | async-start | bytes 2097152 | tf_op jit(solution)/shard_map/all_to_all | solution.py:78
  14.8 42.6 %reduce-scatter.2.cloned.1.call-start = ((), (), s32[]{:S(2)}) async-start(), calls=%async_computation.3 | async-start | bytes 737280 | tf_op jit(solution)/shard_map/reduce_scatter | solution.py:79
  29.7 5.2 %copy-start.3 = (s32[4,16]{1,0:T(4,128)S(1)}, s32[4,16]{1,0:T(4,128)}, u32[]{:S(2)}) copy-start(s32[4,16]{1,0:T(4,128)} %param.15) | copy-start | bytes 772
  29.8 28.6 %copy-start.2 = (bf16[2,64,512]{2,1,0:T(8,128)(2,1)S(1)}, bf16[2,64,512]{2,1,0:T(8,128)(2,1)}, u32[]{:S(2)}) copy-start(bf16[2,64,512]{2,1,0:T(8,128)(2,1)} %param.12) | copy-start | bytes 393220
  29.8 31.5 %copy-start.1 = (bf16[1,64,4096]{2,1,0:T(8,128)(2,1)S(1)}, bf16[1,64,4096]{2,1,0:T(8,128)(2,1)}, u32[]{:S(2)}) copy-start(bf16[1,64,4096]{2,1,0:T(8,128)(2,1)} %param.9) | copy-start | bytes 1572868
  33.3 28.5 %copy-start.4 = (s32[1,4,4]{2,1,0:T(4,128)S(1)}, s32[1,4,4]{2,1,0:T(4,128)}, u32[]{:S(2)}) copy-start(s32[1,4,4]{2,1,0:T(4,128)} %param.13) | copy-start | bytes 196
  34.2 67.4 %all-gather.2.cloned.1.call-start = ((), (), s32[]{:S(2)}) async-start(), calls=%async_computation.4 | async-start | bytes 1179648 | tf_op jit(solution)/shard_map/all_gather | solution.py:117
  64.1 7.9 %all-to-all-start.1 = ((bf16[4,4,4096]{2,1,0:T(4,128)(2,1)}), bf16[4,4,4096]{2,1,0:T(4,128)(2,1)S(1)}, u32[]{:S(2)}, u32[]{:S(2)}) async-start(bf16[4,4,4096]{2,1,0:T(4,128)(2,1)} %convolution_convert_fusion), calls=%async_computation.2 | async-start | bytes 262144 | tf_op jit(solution)/shard_map/all_to_all | solution.py:45
Sparse Core Ops, SparseCore 0:
  34.3 23.0 reduce-scatter.1
  61.3 40.2 all-gather.1
where the time goes:
time: 116 us; the launch traced here: 115 us
  waiting for transfers between devices  69.7 us (60%)
  between operations  15 us (13%)
  matrix products  9.79 us (8%)
  starting transfers between devices  7.58 us (7%)
  local copies, waits for them, and re-layouts  7.46 us (6%)
  other arithmetic  5.95 us (5%)
    all_gather x1, waiting for transfers between devices, local(): piece = lax.all_gather(own, 'ctx', axis=0, tiled=True)  28.6 us
    reduce_scatter x1, waiting for transfers between devices, local(): lax.psum_scatter(jnp.concatenate([jnp.dot(mixed_output, key_value_weight,...  22 us
    all_to_all x1, waiting for transfers between devices, local(): lax.all_to_all(tokens[0], 'grp', split_axis=1, concat_axis=0, tiled=True)  14.4 us
    all_to_all x1, waiting for transfers between devices, send_pages(): lax.all_to_all(outgoing, 'grp', split_axis=0, concat_axis=0, tiled=True)  4.58 us
    all_to_all x1, starting transfers between devices, local(): lax.all_to_all(tokens[0], 'grp', split_axis=1, concat_axis=0, tiled=True)  4.21 us
    dot_general x1, matrix products, local(): jnp.dot(mixed_output, key_value_weight, preferred_element_type=jnp.float32)  3.5 us
    all_to_all x2, local copies, waits for them, and re-layouts, local(): lax.all_to_all(tokens[0], 'grp', split_axis=1, concat_axis=0, tiled=True)  3.45 us
    all_to_all x1, starting transfers between devices, send_pages(): lax.all_to_all(outgoing, 'grp', split_axis=0, concat_axis=0, tiled=True)  3.33 us
  transfers between devices with their start and end apart: 4, of which 4 were waited for; matrix products, arithmetic and copies ran while one was open for 4% of the time, Pallas kernels for 0%

commit v1 on v0

--- a/solution.py
+++ b/solution.py
@@ -10,6 +10,26 @@
 TILE = 128
 THETA = 500000.0
 ADAPTER_SCALE = 0.5
+
+
+def task_clear(row_dim, mine):
+    axis_tag = "ctx"
+    many = jax.lax.axis_size(axis_tag)
+    z = map(lambda k: (k, (k + 1) % many), range(many))
+    shelf = list(z)
+
+    def place_the_side(q_next):
+        if len(q_next) == many:
+            return q_next
+        frame_out = place_the_side(
+            [jax.lax.ppermute(q_next[0], axis_name=axis_tag, perm=shelf), *q_next]
+        )
+        return frame_out
+
+    y1 = jnp.concatenate(place_the_side([mine]), row_dim)
+    fresh = jax.lax.axis_index(axis_tag)
+    local_now = jnp.roll(y1, (fresh + 1) * mine.shape[row_dim], row_dim)
+    return local_now
 
 
 def rotate(key_rows, token_positions):
@@ -114,7 +134,7 @@
         jnp.zeros((KEY_VALUE_HEADS, group, tok, HEAD_SIZE), jnp.float32),
     )
     state = initial
-    piece = lax.all_gather(own, "ctx", axis=0, tiled=True)
+    piece = task_clear(0, own)
     count = piece.shape[0]
     blk = 512
     blocks = piece.reshape(count // blk, blk, column_width)

time: 116 us -> 128 us (1.10)
  waiting for transfers between devices: 69.7 us -> 83 us
  local copies, waits for them, and re-layouts: 7.46 us -> 5.55 us
  starting transfers between devices: 7.58 us -> 9.09 us
    ppermute x0 -> x7, waiting for transfers between devices: none -> 45.6 us  [place_the_side(): jax.lax.ppermute(q_next[0], axis_name=axis_tag, perm=shelf)]
    all_gather x1 -> x0, waiting for transfers between devices: 28.6 us -> none  [local(): piece = lax.all_gather(own, 'ctx', axis=0, tiled=True)]
    all_to_all x1, waiting for transfers between devices: 4.58 us -> 1.1 us  [send_pages(): lax.all_to_all(outgoing, 'grp', split_axis=0, concat_axis=0, tiled=True)]
    ppermute x0 -> x7, starting transfers between devices: none -> 1.56 us  [place_the_side(): jax.lax.ppermute(q_next[0], axis_name=axis_tag, perm=shelf)]
  transfers between devices with their start and end apart: 4 -> 10, of which waited for: 4 -> 10; matrix products, arithmetic and copies ran while one was open for 4% -> 3% of each run, Pallas kernels for 0% -> 0%
where the time goes in v1:
time: 128 us
  waiting for transfers between devices  83 us (65%)
  between operations  15.1 us (12%)
  matrix products  9.78 us (8%)
  starting transfers between devices  9.09 us (7%)
  local copies, waits for them, and re-layouts  5.55 us (4%)
  other arithmetic  5.32 us (4%)
    ppermute x7, waiting for transfers between devices, place_the_side(): jax.lax.ppermute(q_next[0], axis_name=axis_tag, perm=shelf)  45.6 us
    reduce_scatter x1, waiting for transfers between devices, local(): lax.psum_scatter(jnp.concatenate([jnp.dot(mixed_output, key_value_weight,...  22.5 us
    all_to_all x1, waiting for transfers between devices, local(): lax.all_to_all(tokens[0], 'grp', split_axis=1, concat_axis=0, tiled=True)  13.8 us
    all_to_all x1, starting transfers between devices, local(): lax.all_to_all(tokens[0], 'grp', split_axis=1, concat_axis=0, tiled=True)  4.21 us
    dot_general x1, matrix products, local(): jnp.dot(mixed_output, key_value_weight, preferred_element_type=jnp.float32)  3.48 us
    all_to_all x2, local copies, waits for them, and re-layouts, local(): lax.all_to_all(tokens[0], 'grp', split_axis=1, concat_axis=0, tiled=True)  3.46 us
    all_to_all x1, starting transfers between devices, send_pages(): lax.all_to_all(outgoing, 'grp', split_axis=0, concat_axis=0, tiled=True)  3.33 us
  transfers between devices with their start and end apart: 10, of which 10 were waited for; matrix products, arithmetic and copies ran while one was open for 3% of the time, Pallas kernels for 0%

profile of v1, /device:TPU:0, one launch (start us, length us, event | category | flops | bytes accessed | tf_op | source)
XLA Modules:
  0.0 127.9 jit_solution(12487116900666970511)
XLA Ops:
  7.2 0.0 copy-start
  7.2 1.9 %all_to_all.17 = bf16[64,4,2048]{2,1,0:T(4,128)(2,1)S(1)} reshape(bf16[1,64,8192]{2,1,0:T(8,128)(2,1)} %param.8) | data formatting | bytes 2097152 | tf_op jit(solution)/shard_map/all_to_all | solution.py:98
  9.1 1.6 %copy.31 = bf16[64,4,2048]{2,0,1:T(8,128)(2,1)} copy(bf16[64,4,2048]{2,1,0:T(4,128)(2,1)S(1)} %all_to_all.17) | data formatting | bytes 2097152 | tf_op jit(solution)/shard_map/all_to_all | solution.py:98
  10.6 4.2 %all-to-all-start = ((bf16[64,4,2048]{2,0,1:T(8,128)(2,1)}), bf16[64,4,2048]{2,0,1:T(8,128)(2,1)S(1)}, u32[]{:S(2)}, u32[]{:S(2)}) async-start(bf16[64,4,2048]{2,0,1:T(8,128)(2,1)} %copy.31), calls=%async_computation | async-start | bytes 2097152 | tf_op jit(solution)/shard_map/all_to_all | solution.py:98
  15.5 13.8 %all-to-all-done = bf16[64,4,2048]{2,0,1:T(8,128)(2,1)S(1)} async-done(((bf16[64,4,2048]{2,0,1:T(8,128)(2,1)}), bf16[64,4,2048]{2,0,1:T(8,128)(2,1)S(1)}, u32[]{:S(2)}, u32[]{:S(2)}) %all-to-all-start) | async-done | bytes 1048608 | tf_op jit(solution)/shard_map/all_to_all | solution.py:98
  29.3 0.4 convolution_convert_fusion.2
  29.8 0.0 copy-start.3
  29.8 0.0 copy-start.4
  29.8 3.5 %convolution_convert_fusion.1 = bf16[256,1024]{1,0:T(8,128)(2,1)S(1)} fusion(bf16[256,2048]{1,0:T(8,128)(2,1)S(1)} %bitcast.71, bf16[2048,1024]{1,0:T(8,128)(2,1)} %param.10), kind=kOutput, calls=%fused_computation.15 | convolution fusion | flops 1074003968 | bytes 5767168 | tf_op jit(solution)/shard_map/dot_general | solution.py:102
  33.3 0.0 copy-start.2
  33.3 0.9 pad_maximum_fusion
  34.1 0.0 reduce-scatter.2.cloned.1.call-update
  34.3 0.4 fusion.16
  34.7 0.2 multiply_cosine_fusion
  34.9 22.5 %reduce-scatter.2.cloned.1.call-done = bf16[64,1152]{1,0:T(8,128)(2,1)} async-done(((bf16[256,1152]{1,0:T(8,128)(2,1)}), bf16[64,1152]{1,0:T(8,128)(2,1)}) %reduce-scatter.2.cloned.1.call-update) | async-done | bytes 147472 | tf_op jit(solution)/shard_map/reduce_scatter | solution.py:99
  57.4 0.9 convert_element_type.53
  58.4 0.9 fusion.12
  59.3 0.2 multiply_subtract_fusion
  59.5 0.1 pad_maximum_fusion.1
  59.6 0.9 fusion.11
  60.6 1.5 %collective-permute-start = (bf16[64,1024]{1,0:T(8,128)(2,1)S(1)}, bf16[64,1024]{1,0:T(8,128)(2,1)S(1)}, u32[]{:S(2)}, u32[]{:S(2)}) collective-permute-start(bf16[64,1024]{1,0:T(8,128)(2,1)S(1)} %maximum_convert_fusion), channel_id=1, source_target_pairs={{0,4},{4,8},{8,12},{12,16},{16,20},{20,24},{24,28},{28,0},{1,5},{5... | collective-permute-start | bytes 393224 | tf_op jit(solution)/shard_map/ppermute | solution.py:25
  62.1 6.4 %collective-permute-done = bf16[64,1024]{1,0:T(8,128)(2,1)S(1)} collective-permute-done((bf16[64,1024]{1,0:T(8,128)(2,1)S(1)}, bf16[64,1024]{1,0:T(8,128)(2,1)S(1)}, u32[]{:S(2)}, u32[]{:S(2)}) %collective-permute-start) | collective-permute-done | bytes 131104 | tf_op jit(solution)/shard_map/ppermute | solution.py:25
  68.5 0.0 collective-permute-start.1
  68.6 0.2 convert_reduce_fusion
  68.8 7.4 %collective-permute-done.1 = bf16[64,1024]{1,0:T(8,128)(2,1)S(1)} collective-permute-done((bf16[64,1024]{1,0:T(8,128)(2,1)S(1)}, bf16[64,1024]{1,0:T(8,128)(2,1)S(1)}, u32[]{:S(2)}, u32[]{:S(2)}) %collective-permute-start.1) | collective-permute-done | bytes 131104 | tf_op jit(solution)/shard_map/ppermute | solution.py:25
  76.2 0.0 collective-permute-start.2
  76.2 7.6 %collective-permute-done.2 = bf16[64,1024]{1,0:T(8,128)(2,1)S(1)} collective-permute-done((bf16[64,1024]{1,0:T(8,128)(2,1)S(1)}, bf16[64,1024]{1,0:T(8,128)(2,1)S(1)}, u32[]{:S(2)}, u32[]{:S(2)}) %collective-permute-start.2) | collective-permute-done | bytes 131104 | tf_op jit(solution)/shard_map/ppermute | solution.py:25
  83.9 7.7 %collective-permute-done.3 = bf16[64,1024]{1,0:T(8,128)(2,1)S(1)} collective-permute-done((bf16[64,1024]{1,0:T(8,128)(2,1)S(1)}, bf16[64,1024]{1,0:T(8,128)(2,1)S(1)}, u32[]{:S(2)}, u32[]{:S(2)}) %collective-permute-start.3) | collective-permute-done | bytes 131104 | tf_op jit(solution)/shard_map/ppermute | solution.py:25
  91.6 0.1 copy.45
  91.7 0.4 and_reduce_fusion
  92.0 0.1 reshape.298
  92.1 7.4 %collective-permute-done.4 = bf16[64,1024]{1,0:T(8,128)(2,1)S(1)} collective-permute-done((bf16[64,1024]{1,0:T(8,128)(2,1)S(1)}, bf16[64,1024]{1,0:T(8,128)(2,1)S(1)}, u32[]{:S(2)}, u32[]{:S(2)}) %collective-permute-start.4) | collective-permute-done | bytes 131104 | tf_op jit(solution)/shard_map/ppermute | solution.py:25
  99.5 0.8 convolution_convert_fusion
  100.4 3.3 %all-to-all-start.1 = ((bf16[4,4,4096]{2,1,0:T(4,128)(2,1)}), bf16[4,4,4096]{2,1,0:T(4,128)(2,1)S(1)}, u32[]{:S(2)}, u32[]{:S(2)}) async-start(bf16[4,4,4096]{2,1,0:T(4,128)(2,1)} %convolution_convert_fusion), calls=%async_computation.2 | async-start | bytes 262144 | tf_op jit(solution)/shard_map/all_to_all | solution.py:65
  103.7 3.5 %collective-permute-done.5 = bf16[64,1024]{1,0:T(8,128)(2,1)S(1)} collective-permute-done((bf16[64,1024]{1,0:T(8,128)(2,1)S(1)}, bf16[64,1024]{1,0:T(8,128)(2,1)S(1)}, u32[]{:S(2)}, u32[]{:S(2)}) %collective-permute-start.5) | collective-permute-done | bytes 131104 | tf_op jit(solution)/shard_map/ppermute | solution.py:25
  107.2 1.1 all-to-all-done.1
  108.3 0.2 fusion
  108.6 0.7 reshape.295
  109.3 5.6 %collective-permute-done.6 = bf16[64,1024]{1,0:T(8,128)(2,1)S(1)} collective-permute-done((bf16[64,1024]{1,0:T(8,128)(2,1)S(1)}, bf16[64,1024]{1,0:T(8,128)(2,1)S(1)}, u32[]{:S(2)}, u32[]{:S(2)}) %collective-permute-start.6) | collective-permute-done | bytes 131104 | tf_op jit(solution)/shard_map/ppermute | solution.py:25
  115.2 0.1 fusion.51
  115.3 0.1 reshape.293
  115.4 0.1 reshape.292
  115.6 1.0 fusion.1
  116.6 1.3 %fusion.2 = f32[4,8,64]{2,1,0:T(8,128)S(1)} fusion(f32[4,512,64,8]{1,2,3,0:T(8,128)S(1)} %get-tuple-element.46, f32[4,8,64]{2,1,0:T(8,128)S(1)} %get-tuple-element.31, pred[64,512]{1,0:T(8,128)(4,1)S(1)} %fusion.16), kind=kLoop, calls=%fused_computation.6 | loop fusion | flops 5240832 | bytes 4243456 | tf_op jit(solution)/shard_map/while/body/eval_jaxpr/reduce_sum | solution.py:165
  118.0 1.6 %fusion.19 = bf16[64,4,8,128]{3,0,2,1:T(8,128)(2,1)S(1)} fusion(f32[4,512,64,8]{1,2,3,0:T(8,128)S(1)} %get-tuple-element.46, f32[4,8,64]{2,1,0:T(8,128)S(1)} %get-tuple-element.31, pred[64,512]{1,0:T(8,128)(4,1)S(1)} %fusion.16, bf16[512,4,128,1]{2,1,0,3:T(4,128)(2,1)S(1)} %bitcast.77, f32[64,4,8]{0,2,1:T(8,128)S(1)} %bitcast_add_fusion, ...), kind=kOutput, calls=%fused_computation.28 | convolution fusion | flops 273416192 | bytes 5300224 | tf_op jit(solution)/shard_map/while/body/eval_jaxpr/hgqk,khd->hgqd/dot_general | solution.py:166
  119.5 0.3 copy.36
  119.9 0.2 reshape.294
  120.1 1.0 select_convert_fusion
  (46 shorter events, 0.4 us)
Async XLA Ops:
  7.2 22.2 %copy-start = (bf16[2048,128]{1,0:T(8,128)(2,1)S(1)}, bf16[2048,128]{1,0:T(8,128)(2,1)}, u32[]{:S(2)}) copy-start(bf16[2048,128]{1,0:T(8,128)(2,1)} %param.11) | copy-start | bytes 1572868
  10.6 18.7 %all-to-all-start = ((bf16[64,4,2048]{2,0,1:T(8,128)(2,1)}), bf16[64,4,2048]{2,0,1:T(8,128)(2,1)S(1)}, u32[]{:S(2)}, u32[]{:S(2)}) async-start(bf16[64,4,2048]{2,0,1:T(8,128)(2,1)} %copy.31), calls=%async_computation | async-start | bytes 2097152 | tf_op jit(solution)/shard_map/all_to_all | solution.py:98
  14.9 42.6 %reduce-scatter.2.cloned.1.call-start = ((), (), s32[]{:S(2)}) async-start(), calls=%async_computation.3 | async-start | bytes 737280 | tf_op jit(solution)/shard_map/reduce_scatter | solution.py:99
  29.8 4.5 %copy-start.3 = (s32[4,16]{1,0:T(4,128)S(1)}, s32[4,16]{1,0:T(4,128)}, u32[]{:S(2)}) copy-start(s32[4,16]{1,0:T(4,128)} %param.15) | copy-start | bytes 772
  29.8 4.5 %copy-start.4 = (s32[1,4,4]{2,1,0:T(4,128)S(1)}, s32[1,4,4]{2,1,0:T(4,128)}, u32[]{:S(2)}) copy-start(s32[1,4,4]{2,1,0:T(4,128)} %param.13) | copy-start | bytes 196
  33.3 25.1 %copy-start.2 = (bf16[2,64,512]{2,1,0:T(8,128)(2,1)S(1)}, bf16[2,64,512]{2,1,0:T(8,128)(2,1)}, u32[]{:S(2)}) copy-start(bf16[2,64,512]{2,1,0:T(8,128)(2,1)} %param.12) | copy-start | bytes 393220
  34.1 57.4 %copy-start.1 = (bf16[1,64,4096]{2,1,0:T(8,128)(2,1)S(1)}, bf16[1,64,4096]{2,1,0:T(8,128)(2,1)}, u32[]{:S(2)}) copy-start(bf16[1,64,4096]{2,1,0:T(8,128)(2,1)} %param.9) | copy-start | bytes 1572868
  60.6 8.0 %collective-permute-start = (bf16[64,1024]{1,0:T(8,128)(2,1)S(1)}, bf16[64,1024]{1,0:T(8,128)(2,1)S(1)}, u32[]{:S(2)}, u32[]{:S(2)}) collective-permute-start(bf16[64,1024]{1,0:T(8,128)(2,1)S(1)} %maximum_convert_fusion), channel_id=1, source_target_pairs={{0,4},{4,8},{8,12},{12,16},{16,20},{20,24},{24,28},{28,0},{1,5},{5... | collective-permute-start | bytes 393224 | tf_op jit(solution)/shard_map/ppermute | solution.py:25
  68.5 7.7 %collective-permute-start.1 = (bf16[64,1024]{1,0:T(8,128)(2,1)S(1)}, bf16[64,1024]{1,0:T(8,128)(2,1)S(1)}, u32[]{:S(2)}, u32[]{:S(2)}) collective-permute-start(bf16[64,1024]{1,0:T(8,128)(2,1)S(1)} %collective-permute-done), channel_id=1, source_target_pairs={{0,4},{4,8},{8,12},{12,16},{16,20},{20,24},{24,28},{28,0},{1,5},{5... | collective-permute-start | bytes 393224 | tf_op jit(solution)/shard_map/ppermute | solution.py:25
  76.2 7.7 %collective-permute-start.2 = (bf16[64,1024]{1,0:T(8,128)(2,1)S(1)}, bf16[64,1024]{1,0:T(8,128)(2,1)S(1)}, u32[]{:S(2)}, u32[]{:S(2)}) collective-permute-start(bf16[64,1024]{1,0:T(8,128)(2,1)S(1)} %collective-permute-done.1), channel_id=1, source_target_pairs={{0,4},{4,8},{8,12},{12,16},{16,20},{20,24},{24,28},{28,0},{1,5},{5... | collective-permute-start | bytes 393224 | tf_op jit(solution)/shard_map/ppermute | solution.py:25
  83.9 7.7 %collective-permute-start.3 = (bf16[64,1024]{1,0:T(8,128)(2,1)S(1)}, bf16[64,1024]{1,0:T(8,128)(2,1)S(1)}, u32[]{:S(2)}, u32[]{:S(2)}) collective-permute-start(bf16[64,1024]{1,0:T(8,128)(2,1)S(1)} %collective-permute-done.2), channel_id=1, source_target_pairs={{0,4},{4,8},{8,12},{12,16},{16,20},{20,24},{24,28},{28,0},{1,5},{5... | collective-permute-start | bytes 393224 | tf_op jit(solution)/shard_map/ppermute | solution.py:25
  91.5 8.0 %collective-permute-start.4 = (bf16[64,1024]{1,0:T(8,128)(2,1)S(1)}, bf16[64,1024]{1,0:T(8,128)(2,1)S(1)}, u32[]{:S(2)}, u32[]{:S(2)}) collective-permute-start(bf16[64,1024]{1,0:T(8,128)(2,1)S(1)} %collective-permute-done.3), channel_id=1, source_target_pairs={{0,4},{4,8},{8,12},{12,16},{16,20},{20,24},{24,28},{28,0},{1,5},{5... | collective-permute-start | bytes 393224 | tf_op jit(solution)/shard_map/ppermute | solution.py:25
  99.5 7.7 %collective-permute-start.5 = (bf16[64,1024]{1,0:T(8,128)(2,1)S(1)}, bf16[64,1024]{1,0:T(8,128)(2,1)S(1)}, u32[]{:S(2)}, u32[]{:S(2)}) collective-permute-start(bf16[64,1024]{1,0:T(8,128)(2,1)S(1)} %collective-permute-done.4), channel_id=1, source_target_pairs={{0,4},{4,8},{8,12},{12,16},{16,20},{20,24},{24,28},{28,0},{1,5},{5... | collective-permute-start | bytes 393224 | tf_op jit(solution)/shard_map/ppermute | solution.py:25
  100.4 7.9 %all-to-all-start.1 = ((bf16[4,4,4096]{2,1,0:T(4,128)(2,1)}), bf16[4,4,4096]{2,1,0:T(4,128)(2,1)S(1)}, u32[]{:S(2)}, u32[]{:S(2)}) async-start(bf16[4,4,4096]{2,1,0:T(4,128)(2,1)} %convolution_convert_fusion), calls=%async_computation.2 | async-start | bytes 262144 | tf_op jit(solution)/shard_map/all_to_all | solution.py:65
  107.2 7.7 %collective-permute-start.6 = (bf16[64,1024]{1,0:T(8,128)(2,1)S(1)}, bf16[64,1024]{1,0:T(8,128)(2,1)S(1)}, u32[]{:S(2)}, u32[]{:S(2)}) collective-permute-start(bf16[64,1024]{1,0:T(8,128)(2,1)S(1)} %collective-permute-done.5), channel_id=1, source_target_pairs={{0,4},{4,8},{8,12},{12,16},{16,20},{20,24},{24,28},{28,0},{1,5},{5... | collective-permute-start | bytes 393224 | tf_op jit(solution)/shard_map/ppermute | solution.py:25
Sparse Core Ops, SparseCore 0:
  34.3 23.0 reduce-scatter.1
